TPU v7x, 32 devices: a whole 2x2x4 slice. The times are simulated.
32 devices in a mesh: tm: 8 (over z, x), video: 4 (over y, core).
Axes of the slice: x: 2, y: 2, z: 4, core: 2. Of those that a mesh axis runs over, the one named last changes fastest.
Arguments:
- frames: bfloat16 [4, 2048, 512], P('video', 'tm'), may hold values from -6 to 6
- dilated_weight: bfloat16 [3, 512, 512], replicated, may hold values from -0.15625 to 0.15625
- dilated_bias: float32 [512], replicated, may hold values from -3 to 3
- head_matrix: bfloat16 [512, 256], replicated, may hold values from -0.25 to 0.25
- narrations: bfloat16 [1024, 256], P('video'), may hold values from -256 to 256
- narration_counts: int32 [4], replicated, may hold values from 128 to 256, as said below
- narration_spans: int32 [4, 256, 2], P('video'), may hold values from 0 to 2048, as said below
Outputs:
- loss: float32 [], replicated
- dil_grad: float32 [3, 512, 512], P(None, 'tm')
- head_grad: float32 [512, 256], P('tm')
- bias_grad: float32 [512], replicated
- input_gradient: bfloat16 [4, 2048, 512], P('video', 'tm')
Inputs may be any that keep to these rules, and one draw needn't show every extreme that they name: `narration_counts`: the number of live narration slots of each video; some video has all 256. Narration j of a video covers frames narration_spans[v, j, 0] up to but excluding narration_spans[v, j, 1], one frame or more, inside the j-th of the 256 equal runs of 8 frames; spans of slots at or above the count are not live.
All inputs are finite; a program needn't handle non-finite values.
Results may differ from a plain program's by a relative error of at most 0.025.
Values may be sent and summed in bfloat16 or wider, within the bound.
A program may use at most 64 MiB of HBM per device.

v0:
```python
import jax
import jax.numpy as jnp
from jax import lax
from jax.sharding import PartitionSpec as P

SHIFT_N = 2


logit_scale = 0.0625


def passed_along(value, axis, steps):
    count = lax.axis_size(axis)
    first, last = (max(0, -steps), min(count, count - steps))
    return lax.ppermute(value, axis, [(source, source + steps) for source in range(first, last)])


def moved(values, offset):
    return passed_along(values, "tm", offset)


def moved_back(values, offset):
    return passed_along(values, "tm", offset)


def contracted_rows(left, right):
    return lax.dot_general(
        left, right, (((0,), (0,)), ((), ())), preferred_element_type=jnp.float32
    )


def contracted_columns(left, right):
    return lax.dot_general(
        left, right, (((1,), (1,)), ((), ())), preferred_element_type=jnp.float32
    )


def per_device(
    frames, dilated_weight, dilated_bias, head_matrix, narrations, narration_counts, narration_spans
):
    present_tap = frames[0]
    length = present_tap.shape[0]
    narr_local = narrations.shape[0]
    preceding_tap = moved(present_tap, SHIFT_N)
    following_tap = moved(present_tap, -SHIFT_N)
    middle_frames = jnp.dot(present_tap, dilated_weight[1], preferred_element_type=jnp.float32)
    hidden_state = (
        middle_frames
        + jnp.dot(preceding_tap, dilated_weight[0], preferred_element_type=jnp.float32)
        + jnp.dot(following_tap, dilated_weight[2], preferred_element_type=jnp.float32)
        + dilated_bias
    )
    layer_out = (present_tap.astype(jnp.float32) + jnp.maximum(hidden_state, 0.0)).astype(
        jnp.bfloat16
    )
    embedded = jnp.dot(layer_out, head_matrix, preferred_element_type=jnp.float32).astype(
        jnp.bfloat16
    )
    every_narr = lax.all_gather(narrations, "video", axis=0, tiled=True)
    scores = logit_scale * contracted_columns(embedded, every_narr)
    slots = jnp.arange(narr_local, dtype=jnp.int32)
    valid = (slots[None, :] < narration_counts[:, None]).reshape(-1)
    masked = jnp.where(valid[None, :], scores, -jnp.inf)
    highest = jnp.max(masked, axis=1, keepdims=True)
    log_total = highest + jnp.log(jnp.sum(jnp.exp(masked - highest), axis=1, keepdims=True))
    video_index = lax.axis_index("video")
    own_count = lax.dynamic_index_in_dim(narration_counts, video_index, 0, keepdims=False)
    spans = narration_spans[0]
    positions = lax.axis_index("tm") * length + jnp.arange(length, dtype=jnp.int32)
    member = (
        (positions[:, None] >= spans[None, :, 0])
        & (positions[:, None] < spans[None, :, 1])
        & (slots[None, :] < own_count)
    ).astype(jnp.float32)
    labeled = jnp.sum(member, axis=1)
    own_start = video_index * narr_local
    own_scores = lax.dynamic_slice_in_dim(scores, own_start, narr_local, 1)
    local_loss = jnp.sum(labeled * log_total[:, 0]) - jnp.sum(member * own_scores)
    span_lengths = jnp.where(slots < own_count, spans[:, 1] - spans[:, 0], 0).astype(jnp.float32)
    label_total = lax.psum(jnp.sum(span_lengths), "video")
    factor = length * lax.axis_size("tm") * lax.axis_size("video") / label_total
    probs = jnp.exp(masked - log_total) * labeled[:, None]
    own_grad = lax.dynamic_slice_in_dim(probs, own_start, narr_local, 1) - member
    score_grad = lax.dynamic_update_slice_in_dim(probs, own_grad, own_start, 1)
    score_grad = (score_grad * factor).astype(jnp.bfloat16)
    embed_grad = (
        logit_scale * jnp.dot(score_grad, every_narr, preferred_element_type=jnp.float32)
    ).astype(jnp.bfloat16)
    head_resident = contracted_rows(layer_out, embed_grad)
    output_gradient = contracted_columns(embed_grad, head_matrix).astype(jnp.bfloat16)
    preactivation_gradient = jnp.where(
        hidden_state > 0.0, output_gradient.astype(jnp.float32), 0.0
    ).astype(jnp.bfloat16)
    received_following = moved_back(preactivation_gradient, -SHIFT_N)
    received_preceding = moved_back(preactivation_gradient, SHIFT_N)
    bias_local = jnp.sum(preactivation_gradient.astype(jnp.float32), axis=0)
    dilated_resident = jnp.stack(
        [
            contracted_rows(preceding_tap, preactivation_gradient),
            contracted_rows(present_tap, preactivation_gradient),
            contracted_rows(following_tap, preactivation_gradient),
        ]
    )
    input_gradient = (
        output_gradient.astype(jnp.float32)
        + contracted_columns(preactivation_gradient, dilated_weight[1])
        + contracted_columns(received_following, dilated_weight[0])
        + contracted_columns(received_preceding, dilated_weight[2])
    )
    loss_total, bias_overall = lax.psum((local_loss, bias_local), ("tm", "video"))
    dilated_complete, head_complete = lax.psum((dilated_resident, head_resident), "video")
    dilated_fraction, head_fraction = (
        lax.psum_scatter(dilated_complete, "tm", scatter_dimension=1, tiled=True),
        lax.psum_scatter(head_complete[None], "tm", scatter_dimension=1, tiled=True),
    )
    loss = loss_total / label_total
    return (
        loss,
        dilated_fraction,
        head_fraction[0],
        bias_overall,
        input_gradient.astype(jnp.bfloat16)[None],
    )


def solution(mesh):
    return jax.shard_map(
        per_device,
        mesh=mesh,
        in_specs=(
            P("video", "tm", None),
            P(),
            P(),
            P(),
            P("video", None),
            P(),
            P("video", None, None),
        ),
        out_specs=(P(), P(None, "tm", None), P("tm", None), P(), P("video", "tm", None)),
        check_vma=False,
    )
```

profile of v0, /device:TPU:0, one launch (start us, length us, event | category | flops | bytes accessed | tf_op | source)
XLA Modules:
  0.0 322.5 jit_solution(6570510090301693052)
XLA Ops:
  7.2 1.4 collective-permute-start.1
  8.7 5.6 %collective-permute-start = (bf16[256,512]{1,0:T(8,128)(2,1)}, bf16[256,512]{1,0:T(8,128)(2,1)S(1)}, u32[]{:S(2)}, u32[]{:S(2)}) collective-permute-start(bf16[256,512]{1,0:T(8,128)(2,1)} %bitcast.65), channel_id=1, source_target_pairs={{0,8},{4,12},{8,16},{12,20},{16,24},{20,28},{1,9},{5,13},{9,17},{1... | collective-permute-start | bytes 786440 | tf_op jit(solution)/shard_map/ppermute | solution.py:15
  15.0 1.2 dynamic_slice.10
  17.0 7.8 %all_gather.3 = bf16[1024,256]{1,0:T(8,128)(2,1)S(1)} all-gather(bf16[256,256]{1,0:T(8,128)(2,1)} %param.11), channel_id=1, replica_groups=mesh['tm'=8,'video'=4] {'video'}, dimensions={0}, use_global_device_ids=true | all-gather | bytes 655360 | tf_op jit(solution)/shard_map/all_gather | solution.py:59
  24.9 1.2 convert_reduce_fusion.2
  26.8 7.1 %psum.36 = f32[]{:T(128)} all-reduce(f32[]{:T(128)} %convert_reduce_fusion.2), channel_id=1, replica_groups=mesh['tm'=8,'video'=4] {'video'}, use_global_device_ids=true, to_apply=%region_7.8 | all-reduce | flops 1 | bytes 8 | tf_op jit(solution)/shard_map/psum | solution.py:80
  34.5 1.4 fusion.12
  36.3 1.3 fusion.1
  38.6 0.8 select_reduce_fusion.1
  40.7 1.1 convert_reduce_fusion
  42.1 1.3 convolution_bitcast_fusion
  44.1 3.5 %copy.13 = f32[3,512,512]{2,0,1:T(4,128)} copy(f32[3,512,512]{1,2,0:T(8,128)S(1)} %pad_maximum_fusion) | data formatting | bytes 6291456 | tf_op jit(solution)/shard_map/stack | solution.py:97
  47.7 1.0 copy-done.2
  48.8 1.1 convolution_bitcast_fusion.3
  51.3 1.3 collective-permute-start.2
  52.6 4.6 %collective-permute-start.3 = (bf16[256,512]{1,0:T(8,128)(2,1)S(1)}, bf16[256,512]{1,0:T(8,128)(2,1)S(1)}, u32[]{:S(2)}, u32[]{:S(2)}) collective-permute-start(bf16[256,512]{1,0:T(8,128)(2,1)S(1)} %copy-done.4), channel_id=1, source_target_pairs={{0,8},{4,12},{8,16},{12,20},{16,24},{20,28},{1,9},{5,13},{9,17},{1... | collective-permute-start | bytes 786440 | tf_op jit(solution)/shard_map/ppermute | solution.py:15
  58.4 45.7 %all-reduce.1 = (f32[]{:T(128)}, f32[512]{0:T(512)}) all-reduce(f32[]{:T(128)S(6)} %sub.27, f32[512]{0:T(512)S(1)} %get-tuple-element.21), channel_id=1, replica_groups=mesh['tm'=8,'video'=4] {'tm','video'}, use_global_device_ids=true, to_apply=%region_5.6 | all-reduce | flops 513 | bytes 4104 | tf_op jit(solution)/shard_map/psum | solution.py:110
  105.8 105.3 %all-reduce.6.cloned.1.call-done = f32[3,512,512]{2,0,1:T(4,128)} async-done(((f32[3,512,512]{2,0,1:T(4,128)}), f32[3,512,512]{2,0,1:T(4,128)}) %all-reduce.6.cloned.1.call-update) | async-done | bytes 3145744
  211.1 1.9 constant_dynamic-slice_fusion
  213.1 63.1 %reduce-scatter.2.cloned.1.call-done = f32[1,64,256]{2,1,0:T(8,128)} async-done(((f32[1,512,256]{2,1,0:T(8,128)}), f32[1,64,256]{2,1,0:T(8,128)}) %reduce-scatter.2.cloned.1.call-update) | async-done | bytes 65552 | tf_op jit(solution)/shard_map/reduce_scatter | solution.py:114
  276.5 2.0 fusion.4
  278.5 33.0 %all-reduce.8.cloned.1.call-done = (f32[3,64,512]{2,0,1:T(4,128)}, f32[1,64,256]{2,1,0:T(8,128)}) async-done(((f32[3,64,512]{2,0,1:T(4,128)}, f32[1,64,256]{2,1,0:T(8,128)}), (f32[3,64,512]{2,0,1:T(4,128)}, f32[1,64,256]{2,1,0:T(8,128)})) %all-reduce.8.cloned.1.call-update) | async-done | bytes 458768 | tf_op jit(solution)/shard_map/psum | solution.py:111
  311.5 1.9 copy.14
  313.4 1.5 copy.19
  (51 shorter events, 7.2 us)
Async XLA Ops:
  7.2 30.4 %copy-start = (bf16[512,256]{1,0:T(8,128)(2,1)S(1)}, bf16[512,256]{1,0:T(8,128)(2,1)}, u32[]{:S(2)}) copy-start(bf16[512,256]{1,0:T(8,128)(2,1)} %param.10) | copy-start | bytes 786436
  7.2 28.8 %copy-start.5 = (bf16[3,512,512]{2,1,0:T(8,128)(2,1)S(1)}, bf16[3,512,512]{2,1,0:T(8,128)(2,1)}, u32[]{:S(2)}) copy-start(bf16[3,512,512]{2,1,0:T(8,128)(2,1)} %param.8) | copy-start | bytes 4718596
  7.2 203.9 %all-reduce.6.cloned.1.call-start = ((), (), s32[]{:S(2)}) async-start(), calls=%async_computation.2 | async-start | bytes 8388608
  7.2 29.1 %collective-permute-start.1 = (bf16[256,512]{1,0:T(8,128)(2,1)}, bf16[256,512]{1,0:T(8,128)(2,1)}, u32[]{:S(2)}, u32[]{:S(2)}) collective-permute-start(bf16[256,512]{1,0:T(8,128)(2,1)} %bitcast.64), channel_id=1, source_target_pairs={{8,0},{12,4},{16,8},{20,12},{24,16},{28,20},{9,1},{13,5},{17,9},{2... | collective-permute-start | bytes 786440 | tf_op jit(solution)/shard_map/ppermute | solution.py:15
  8.7 27.3 %collective-permute-start = (bf16[256,512]{1,0:T(8,128)(2,1)}, bf16[256,512]{1,0:T(8,128)(2,1)S(1)}, u32[]{:S(2)}, u32[]{:S(2)}) collective-permute-start(bf16[256,512]{1,0:T(8,128)(2,1)} %bitcast.65), channel_id=1, source_target_pairs={{0,8},{4,12},{8,16},{12,20},{16,24},{20,28},{1,9},{5,13},{9,17},{1... | collective-permute-start | bytes 786440 | tf_op jit(solution)/shard_map/ppermute | solution.py:15
  34.5 1.8 copy-start.10
  36.0 1.6 copy-start.7
  37.6 3.1 copy-start.1
  41.8 1.6 copy-start.3
  47.6 1.1 copy-start.2
  47.6 1.2 copy-start.8
  47.6 57.9 %copy-start.9 = (f32[256,512]{1,0:T(8,128)S(1)}, f32[256,512]{1,0:T(8,128)}, u32[]{:S(2)}) copy-start(f32[256,512]{1,0:T(8,128)} %get-tuple-element.29) | copy-start | bytes 1572868
  47.6 2.4 copy-start.11
  47.6 3.6 %copy-start.4 = (bf16[256,512]{1,0:T(8,128)(2,1)S(1)}, bf16[256,512]{1,0:T(8,128)(2,1)}, u32[]{:S(2)}) copy-start(bf16[256,512]{1,0:T(8,128)(2,1)} %copy-done.3) | copy-start | bytes 786436
  47.6 57.9 %copy-start.6 = (bf16[3,512,512]{2,1,0:T(8,128)(2,1)S(1)}, bf16[3,512,512]{2,1,0:T(8,128)(2,1)}, u32[]{:S(2)}) copy-start(bf16[3,512,512]{2,1,0:T(8,128)(2,1)} %param.8) | copy-start | bytes 4718596
  47.6 228.5 %reduce-scatter.2.cloned.1.call-start = ((), (), s32[]{:S(2)}) async-start(), calls=%async_computation.1 | async-start | bytes 589824 | tf_op jit(solution)/shard_map/reduce_scatter | solution.py:114
  49.9 261.5 %all-reduce.8.cloned.1.call-start = ((), (), s32[]{:S(2)}) async-start(), calls=%async_computation.3 | async-start | bytes 1179648 | tf_op jit(solution)/shard_map/psum | solution.py:111
  51.3 225.2 %collective-permute-start.2 = (bf16[256,512]{1,0:T(8,128)(2,1)S(1)}, bf16[256,512]{1,0:T(8,128)(2,1)}, u32[]{:S(2)}, u32[]{:S(2)}) collective-permute-start(bf16[256,512]{1,0:T(8,128)(2,1)S(1)} %copy-done.4), channel_id=1, source_target_pairs={{8,0},{12,4},{16,8},{20,12},{24,16},{28,20},{9,1},{13,5},{17,9},{2... | collective-permute-start | bytes 786440 | tf_op jit(solution)/shard_map/ppermute | solution.py:15
  52.6 223.6 %collective-permute-start.3 = (bf16[256,512]{1,0:T(8,128)(2,1)S(1)}, bf16[256,512]{1,0:T(8,128)(2,1)S(1)}, u32[]{:S(2)}, u32[]{:S(2)}) collective-permute-start(bf16[256,512]{1,0:T(8,128)(2,1)S(1)} %copy-done.4), channel_id=1, source_target_pairs={{0,8},{4,12},{8,16},{12,20},{16,24},{20,28},{1,9},{5,13},{9,17},{1... | collective-permute-start | bytes 786440 | tf_op jit(solution)/shard_map/ppermute | solution.py:15
Sparse Core Ops, SparseCore 0:
  47.7 163.3 all-reduce.5
  214.5 61.6 reduce-scatter.1
  278.6 32.8 all-reduce.7
where the time goes:
time: 323 us
  waiting for transfers between devices  201 us (62%)
  blocking collectives  60.6 us (19%)
  between operations  19.2 us (6%)
  starting transfers between devices  13 us (4%)
  local copies, waits for them, and re-layouts  12.6 us (4%)
  matrix products  10.8 us (3%)
  other arithmetic  5.01 us (2%)
    unnamed x4, waiting for transfers between devices  105 us
    reduce_scatter x1, waiting for transfers between devices, per_device(): lax.psum_scatter(head_complete[None], 'tm', scatter_dimension=1, tiled=True)  63.1 us
    psum x1, blocking collectives, per_device(): lax.psum((local_loss, bias_local), ('tm', 'video'))  45.7 us
    psum x1, waiting for transfers between devices, per_device(): lax.psum((dilated_resident, head_resident), 'video')  33 us
    ppermute x4, starting transfers between devices, passed_along(): lax.ppermute(value, axis, [(source, source + steps) for source in range(f...  12.9 us
    all_gather x1, blocking collectives, per_device(): every_narr = lax.all_gather(narrations, 'video', axis=0, tiled=True)  7.83 us
    psum x1, blocking collectives, per_device(): label_total = lax.psum(jnp.sum(span_lengths), 'video')  7.07 us
    unnamed x28, local copies, waits for them, and re-layouts  7.04 us
  transfers between devices with their start and end apart: 7, of which 3 were waited for; matrix products, arithmetic and copies ran while one was open for 4% of the time, Pallas kernels for 0%

commit v1 on v0

--- a/solution.py
+++ b/solution.py
@@ -1,6 +1,10 @@
+import functools
+
 import jax
 import jax.numpy as jnp
 from jax import lax
+from jax.experimental import pallas as pl
+from jax.experimental.pallas import tpu as pltpu
 from jax.sharding import PartitionSpec as P
 
 SHIFT_N = 2
@@ -123,9 +127,385 @@
     )
 
 
+MESH = pl.DeviceIdType.MESH
+F32, BF16 = jnp.float32, jnp.bfloat16
+
+
+def section_kernel(
+    n, videos, parts,
+    counts_ref, frames_ref, weight_ref, bias_ref, head_ref, narr_ref, spans_ref,
+    dil_ref, head_out_ref, input_ref, small_ref,
+    earlier, later, narr_all, spans_all, hidden, out_grad, pre, pre_next, pre_prev,
+    small_send, small_recv, edge_send, edge_recv, gather_send, gather_recv,
+    small_ssem, small_rsem, *buffers,
+):
+    tm, vid = lax.axis_index("tm"), lax.axis_index("video")
+    runs = n // 2
+    core, row = lax.rem(vid, 2), lax.div(vid, 2)
+    side, deep = lax.rem(tm, 2), lax.div(tm, 2)
+    across_core = {"tm": tm, "video": vid + 1 - 2 * core}
+    across_row = {"tm": tm, "video": lax.rem(vid + 2, videos)}
+    across_side = {"tm": tm + 1 - 2 * side, "video": vid}
+
+    def at_run(step):
+        return {"tm": lax.rem(tm + 2 * step, n), "video": vid}
+
+    def at_video(step):
+        return {"tm": tm, "video": lax.rem(vid + step, videos)}
+
+    barrier = pltpu.get_barrier_semaphore()
+    peers = [across_side] + [at_run(s) for s in range(1, runs)] + [at_video(s) for s in range(1, videos)]
+    for peer in peers:
+        pl.semaphore_signal(barrier, inc=1, device_id=peer, device_id_type=MESH)
+    pl.semaphore_wait(barrier, len(peers))
+
+    def remote(src, dst, ssem, rsem, peer):
+        return pltpu.make_async_remote_copy(
+            src_ref=src, dst_ref=dst, send_sem=ssem, recv_sem=rsem, device_id=peer, device_id_type=MESH
+        )
+
+    has_prev, has_next = tm >= SHIFT_N, tm < n - SHIFT_N
+    up = {"tm": lax.rem(tm + SHIFT_N, n), "video": vid}
+    down = {"tm": lax.rem(tm + n - SHIFT_N, n), "video": vid}
+    frames_up = remote(frames_ref.at[0], earlier, edge_send.at[0], edge_recv.at[0], up)
+    frames_down = remote(frames_ref.at[0], later, edge_send.at[1], edge_recv.at[1], down)
+    pre_up = remote(pre, pre_prev, edge_send.at[2], edge_recv.at[2], up)
+    pre_down = remote(pre, pre_next, edge_send.at[3], edge_recv.at[3], down)
+    pl.when(has_next)(frames_up.start)
+    pl.when(has_prev)(frames_down.start)
+    gathers = []
+    for step in range(1, videos):
+        gathers.append(remote(spans_ref, spans_all.at[step - 1], gather_send.at[0, step - 1], gather_recv.at[0, step - 1], at_video(step)))
+        gathers.append(remote(narr_ref, narr_all.at[step - 1], gather_send.at[1, step - 1], gather_recv.at[1, step - 1], at_video(step)))
+    for copy in gathers:
+        copy.start()
+
+    def no_prev():
+        earlier[...] = jnp.zeros_like(earlier)
+        pre_prev[...] = jnp.zeros_like(pre_prev)
+
+    def no_next():
+        later[...] = jnp.zeros_like(later)
+        pre_next[...] = jnp.zeros_like(pre_next)
+
+    pl.when(jnp.logical_not(has_prev))(no_prev)
+    pl.when(jnp.logical_not(has_next))(no_next)
+
+    present = frames_ref[0]
+    length = present.shape[0]
+    slots_count = narr_ref.shape[0]
+    hidden[...] = jnp.dot(present, weight_ref[1], preferred_element_type=F32) + bias_ref[...]
+    slots = lax.broadcasted_iota(jnp.int32, (1, slots_count), 1)
+    positions = tm * length + lax.broadcasted_iota(jnp.int32, (length, 1), 0)
+    starts, ends = spans_ref[0:1, :], spans_ref[1:2, :]
+    own_live = slots < counts_ref[vid]
+    member = ((positions >= starts) & (positions < ends) & own_live).astype(F32)
+    labeled = jnp.sum(member, axis=1, keepdims=True)
+
+    def recv_up():
+        frames_up.wait_recv()
+
+    pl.when(has_prev)(recv_up)
+    hidden[...] += jnp.dot(earlier[...], weight_ref[0], preferred_element_type=F32)
+    pl.when(has_next)(frames_down.wait_recv)
+    hidden[...] += jnp.dot(later[...], weight_ref[2], preferred_element_type=F32)
+    layer_out = (present.astype(F32) + jnp.maximum(hidden[...], 0.0)).astype(BF16)
+    embedded = jnp.dot(layer_out, head_ref[...], preferred_element_type=F32).astype(BF16)
+
+    span_sum = jnp.where(own_live, (ends - starts).astype(F32), 0.0)
+    narrs, masked = [], []
+    for step in range(videos):
+        if step:
+            gathers[2 * (step - 1)].wait_recv()
+            gathers[2 * (step - 1) + 1].wait_recv()
+            live = slots < counts_ref[lax.rem(vid + videos - step, videos)]
+            lengths = (spans_all[step - 1, 1:2, :] - spans_all[step - 1, 0:1, :]).astype(F32)
+            span_sum = span_sum + jnp.where(live, lengths, 0.0)
+            table = narr_all[step - 1]
+        else:
+            live, table = own_live, narr_ref[...]
+        narrs.append(table)
+        scores = logit_scale * contracted_columns(embedded, table)
+        if step == 0:
+            own_scores = scores
+        masked.append(jnp.where(live, scores, -jnp.inf))
+    label_total = jnp.sum(span_sum, axis=1, keepdims=True)
+    highest = functools.reduce(jnp.maximum, [jnp.max(m, axis=1, keepdims=True) for m in masked])
+    powers = [jnp.exp(m - highest) for m in masked]
+    total = functools.reduce(jnp.add, [jnp.sum(e, axis=1, keepdims=True) for e in powers])
+    log_total = highest + jnp.log(total)
+    local_loss = jnp.sum(labeled * log_total, axis=0, keepdims=True) - jnp.sum(
+        jnp.sum(member * own_scores, axis=1, keepdims=True), axis=0, keepdims=True
+    )
+    factor = (length * n * videos) / label_total
+    weight = labeled / total
+    embed_sum = None
+    for step in range(videos):
+        probs = powers[step] * weight
+        if step == 0:
+            probs = probs - member
+        term = jnp.dot((probs * factor).astype(BF16), narrs[step], preferred_element_type=F32)
+        embed_sum = term if embed_sum is None else embed_sum + term
+    embed_grad = (logit_scale * embed_sum).astype(BF16)
+    out_grad[...] = contracted_columns(embed_grad, head_ref[...]).astype(BF16)
+    pre[...] = jnp.where(hidden[...] > 0.0, out_grad[...].astype(F32), 0.0).astype(BF16)
+    pl.when(has_next)(pre_up.start)
+    pl.when(has_prev)(pre_down.start)
+
+    taps = (earlier, frames_ref.at[0], later)
+    slabs = [buffers[13 * p:13 * (p + 1)] for p in range(len(parts))]
+    band = slabs[0][0].shape[-2]
+
+    def scatter(values, slab, first):
+        accum, sent0 = slab[0], slab[1]
+        width = values.shape[1]
+        for z in range(runs):
+            for x in range(2):
+                for y in range(2):
+                    for c in range(2):
+                        at = (((z * 2 + x) * 2 + y) * 2 + c) * band
+                        accum[c, y, x, z, :, first:first + width] = values[at:at + band]
+
+    def send_first(slab):
+        accum, sent0, recv0 = slab[0], slab[1], slab[2]
+        sent0[...] = accum[1 - core].astype(BF16)
+        copy = remote(sent0, recv0, slab[9].at[0], slab[10].at[0], across_core)
+        copy.start()
+        return copy
+
+    first_copies = []
+    for (pieces, order), slab in zip(parts, slabs):
+        first = 0
+        for tap, low, high in pieces:
+            if tap == 3:
+                values = contracted_rows(layer_out, embed_grad[:, low:high])
+            else:
+                values = contracted_rows(taps[tap][...], pre[:, low:high])
+            scatter(values, slab, first)
+            first += high - low
+        first_copies.append(send_first(slab))
+
+    bias_local = jnp.sum(pre[...].astype(F32), axis=0, keepdims=True)
+    rows = lax.broadcasted_iota(jnp.int32, small_ref.shape, 0)
+    small = jnp.where(rows == 0, bias_local, jnp.where(rows == 1, local_loss, 0.0))
+    small_copies = []
+
+    def small_start(index, peers_of):
+        started = []
+        for k, peer in enumerate(peers_of):
+            copy = remote(small_send.at[index], small_recv.at[index + k], small_ssem.at[index + k], small_rsem.at[index + k], peer)
+            copy.start()
+            started.append(copy)
+        small_copies.extend(started)
+        return started
+
+    small_send[0] = small
+    small_now = small_start(0, [across_core])
+
+    second_copies = []
+    for (pieces, order), slab, copy in zip(parts, slabs, first_copies):
+        accum, recv0, sent1, recv1 = slab[0], slab[2], slab[3], slab[4]
+        copy.wait_recv()
+        if order == "rows":
+            for x in range(2):
+                sent1[x] = (accum[core, 1 - row, x] + recv0[1 - row, x].astype(F32)).astype(BF16)
+            peer = across_row
+        else:
+            for y in range(2):
+                sent1[y] = (accum[core, y, 1 - side] + recv0[y, 1 - side].astype(F32)).astype(BF16)
+            peer = across_side
+        copy = remote(sent1, recv1, slab[9].at[1], slab[10].at[1], peer)
+        copy.start()
+        second_copies.append(copy)
+    small_now[0].wait_recv()
+    small = small + small_recv[0]
+    small_send[1] = small
+    small_now = small_start(1, [across_row])
+
+    grad = out_grad[...].astype(F32) + contracted_columns(pre[...], weight_ref[1])
+    pl.when(has_prev)(pre_up.wait_recv)
+    grad = grad + contracted_columns(pre_prev[...], weight_ref[2])
+    pl.when(has_next)(pre_down.wait_recv)
+    grad = grad + contracted_columns(pre_next[...], weight_ref[0])
+    input_ref[0] = grad.astype(BF16)
+
+    third_copies = []
+    for (pieces, order), slab, copy in zip(parts, slabs, second_copies):
+        accum, recv0, recv1, sent2, recv2 = slab[0], slab[2], slab[4], slab[5], slab[6]
+        copy.wait_recv()
+        if order == "rows":
+            sent2[...] = (accum[core, row, 1 - side] + recv0[row, 1 - side].astype(F32) + recv1[1 - side].astype(F32)).astype(BF16)
+            peer = across_side
+        else:
+            sent2[...] = (accum[core, 1 - row, side] + recv0[1 - row, side].astype(F32) + recv1[1 - row].astype(F32)).astype(BF16)
+            peer = across_row
+        copy = remote(sent2, recv2, slab[9].at[2], slab[10].at[2], peer)
+        copy.start()
+        third_copies.append(copy)
+    small_now[0].wait_recv()
+    small = small + small_recv[1]
+    small_send[2] = small
+    small_now = small_start(2, [across_side])
+
+    run_copies = []
+    for (pieces, order), slab, copy in zip(parts, slabs, third_copies):
+        accum, recv0, recv1, recv2, sent3, recv3 = slab[0], slab[2], slab[4], slab[6], slab[7], slab[8]
+        copy.wait_recv()
+        kept = recv1.at[side] if order == "rows" else recv1.at[row]
+        started = []
+        for step in range(1, runs):
+            z = lax.rem(deep + step, runs)
+            sent3[step] = (
+                accum[core, row, side, z] + recv0[row, side, z].astype(F32) + kept[z].astype(F32) + recv2[z].astype(F32)
+            ).astype(BF16)
+            copy = remote(sent3.at[step], recv3.at[step], slab[9].at[2 + step], slab[10].at[2 + step], at_run(step))
+            copy.start()
+            started.append(copy)
+        run_copies.append(started)
+    small_now[0].wait_recv()
+    small = small + small_recv[2]
+    small_send[3] = small
+    small_now = small_start(3, [at_run(s) for s in range(1, runs)])
+
+    final_copies = []
+    for (pieces, order), slab, started in zip(parts, slabs, run_copies):
+        accum, recv0, recv1, recv2, recv3 = slab[0], slab[2], slab[4], slab[6], slab[8]
+        final, fsend, frecv = slab[11], slab[9], slab[10]
+        final_in = slab[12]
+        kept = recv1.at[side] if order == "rows" else recv1.at[row]
+        value = accum[core, row, side, deep] + recv0[row, side, deep].astype(F32) + kept[deep].astype(F32) + recv2[deep].astype(F32)
+        for step in range(1, runs):
+            started[step - 1].wait_recv()
+            value = value + recv3[step].astype(F32)
+        final[...] = value.astype(BF16)
+        copies = []
+        for step in range(1, videos):
+            index = 1 + runs + step
+            copy = remote(final, final_in.at[step - 1], fsend.at[index], frecv.at[index], at_video(step))
+            copy.start()
+            copies.append(copy)
+        final_copies.append(copies)
+
+    for copy in small_now:
+        copy.wait_recv()
+    total_small = None
+    for z in range(runs):
+        step = lax.rem(deep - z + runs, runs)
+        term = small
+        for s in range(1, runs):
+            term = jnp.where(step == s, small_recv[2 + s], term)
+        total_small = term if total_small is None else total_small + term
+    rows = lax.broadcasted_iota(jnp.int32, small_ref.shape, 0)
+    small_ref[...] = jnp.where(rows == 1, total_small / label_total, total_small)
+
+    for (pieces, order), slab, copies in zip(parts, slabs, final_copies):
+        for step in range(videos):
+            if step:
+                copies[step - 1].wait_recv()
+                value = slab[12][step - 1]
+            else:
+                value = slab[11][...]
+            value = value.astype(F32)
+            at = pl.ds(pl.multiple_of(lax.rem(vid + videos - step, videos) * band, band), band)
+            first = 0
+            for tap, low, high in pieces:
+                piece = value[:, first:first + high - low]
+                if tap == 3:
+                    head_out_ref[at, low:high] = piece
+                else:
+                    dil_ref[tap, at, low:high] = piece
+                first += high - low
+
+    pl.when(has_next)(frames_up.wait_send)
+    pl.when(has_prev)(frames_down.wait_send)
+    pl.when(has_next)(pre_up.wait_send)
+    pl.when(has_prev)(pre_down.wait_send)
+    for copy in gathers + first_copies + small_copies + second_copies + third_copies:
+        copy.wait_send()
+    for started in run_copies + final_copies:
+        for copy in started:
+            copy.wait_send()
+
+
+def section(n, videos, frames, dilated_weight, dilated_bias, head_matrix, narrations, narration_counts, narration_spans):
+    length, channels = frames.shape[1:]
+    width, slots = head_matrix.shape[1], narrations.shape[0]
+    rows, runs = channels // n, n // 2
+    band = rows // videos
+    half, head_half = channels // 2, width // 2
+    parts = tuple(
+        (tuple((tap, p * half, (p + 1) * half) for tap in range(3)) + ((3, p * head_half, (p + 1) * head_half),), order)
+        for p, order in enumerate(("rows", "sides"))
+    )
+    scratch = [
+        pltpu.VMEM((length, channels), BF16),
+        pltpu.VMEM((length, channels), BF16),
+        pltpu.VMEM((videos - 1, slots, width), BF16),
+        pltpu.VMEM((videos - 1, 2, slots), jnp.int32),
+        pltpu.VMEM((length, channels), F32),
+        pltpu.VMEM((length, channels), BF16),
+        pltpu.VMEM((length, channels), BF16),
+        pltpu.VMEM((length, channels), BF16),
+        pltpu.VMEM((length, channels), BF16),
+        pltpu.VMEM((4, 8, channels), F32),
+        pltpu.VMEM((2 + runs, 8, channels), F32),
+        pltpu.SemaphoreType.DMA((4,)),
+        pltpu.SemaphoreType.DMA((4,)),
+        pltpu.SemaphoreType.DMA((2, videos - 1)),
+        pltpu.SemaphoreType.DMA((2, videos - 1)),
+        pltpu.SemaphoreType.DMA((2 + runs,)),
+        pltpu.SemaphoreType.DMA((2 + runs,)),
+    ]
+    for pieces, order in parts:
+        columns = sum(high - low for _, low, high in pieces)
+        scratch += [
+            pltpu.VMEM((2, 2, 2, runs, band, columns), F32),
+            pltpu.VMEM((2, 2, runs, band, columns), BF16),
+            pltpu.VMEM((2, 2, runs, band, columns), BF16),
+            pltpu.VMEM((2, runs, band, columns), BF16),
+            pltpu.VMEM((2, runs, band, columns), BF16),
+            pltpu.VMEM((runs, band, columns), BF16),
+            pltpu.VMEM((runs, band, columns), BF16),
+            pltpu.VMEM((runs, band, columns), BF16),
+            pltpu.VMEM((runs, band, columns), BF16),
+            pltpu.SemaphoreType.DMA((1 + runs + videos,)),
+            pltpu.SemaphoreType.DMA((1 + runs + videos,)),
+            pltpu.VMEM((band, columns), BF16),
+            pltpu.VMEM((videos - 1, band, columns), BF16),
+        ]
+    vmem = pl.BlockSpec(memory_space=pltpu.VMEM)
+    dil, head, inputs, small = pl.pallas_call(
+        functools.partial(section_kernel, n, videos, parts),
+        out_shape=(
+            jax.ShapeDtypeStruct((3, rows, channels), F32),
+            jax.ShapeDtypeStruct((rows, width), F32),
+            jax.ShapeDtypeStruct((1, length, channels), BF16),
+            jax.ShapeDtypeStruct((8, channels), F32),
+        ),
+        in_specs=[pl.BlockSpec(memory_space=pltpu.SMEM)] + [vmem] * 6,
+        out_specs=(vmem,) * 4,
+        scratch_shapes=scratch,
+        compiler_params=pltpu.CompilerParams(
+            collective_id=0, has_side_effects=True, vmem_limit_bytes=48 * 1024 * 1024
+        ),
+    )(
+        narration_counts, frames, dilated_weight, dilated_bias[None], head_matrix, narrations,
+        narration_spans[0].T,
+    )
+    return small[1, 0], dil, head, small[0], inputs
+
+
 def solution(mesh):
+    n, videos = mesh.shape["tm"], mesh.shape["video"]
+
+    def body(*arrays):
+        frames, weight = arrays[0], arrays[1]
+        if videos == 4 and n % 4 == 0 and weight.shape[1] % (16 * n * videos) == 0:
+            return section(n, videos, *arrays)
+        return per_device(*arrays)
+
     return jax.shard_map(
-        per_device,
+        body,
         mesh=mesh,
         in_specs=(
             P("video", "tm", None),

time: 323 us -> 50.4 us (0.16)
  waiting for transfers between devices: 201 us -> 0 us
  blocking collectives: 60.6 us -> 0 us
  Pallas kernels: 0 us -> 40.1 us
  between operations: 19.2 us -> 0.66 us
  starting transfers between devices: 13 us -> 0 us
  matrix products: 10.8 us -> 0 us
  other arithmetic: 5.01 us -> 0 us
    unnamed x4 -> x0, waiting for transfers between devices: 105 us -> none
    reduce_scatter x1 -> x0, waiting for transfers between devices: 63.1 us -> none  [per_device(): lax.psum_scatter(head_complete[None], 'tm', scatter_dimension=1, tiled=True)]
    psum x2 -> x0, blocking collectives: 52.8 us -> none  [the longest x1 45.7 us: per_device(): lax.psum((local_loss, bias_local), ('tm', 'video'))]
    pallas_call x0 -> x1, Pallas kernels: none -> 40.1 us  [section(): pl.pallas_call(functools.partial(section_kernel, n, videos, parts), out_s...]
    psum x1 -> x0, waiting for transfers between devices: 33 us -> none  [per_device(): lax.psum((dilated_resident, head_resident), 'video')]
    ppermute x4 -> x0, starting transfers between devices: 12.9 us -> none  [passed_along(): lax.ppermute(value, axis, [(source, source + steps) for source in range(f...]
    dot_general x13 -> x0, matrix products: 10.8 us -> none  [the longest x5 4.39 us: contracted_columns(): lax.dot_general(left, right, (((1,), (1,)), ((), ())), preferred_element_...]
    all_gather x1 -> x0, blocking collectives: 7.83 us -> none  [per_device(): every_narr = lax.all_gather(narrations, 'video', axis=0, tiled=True)]
  transfers between devices with their start and end apart: 7 -> 0, of which waited for: 3 -> 0; matrix products, arithmetic and copies ran while one was open for 4% -> 0% of each run, Pallas kernels for 0% -> 0%
where the time goes in v1:
time: 50.4 us; the launch traced here: 50.2 us
  Pallas kernels  40.1 us (80%)
  local copies, waits for them, and re-layouts  9.39 us (19%)
  between operations  0.66 us (1%)
    pallas_call x1, Pallas kernels, section(): pl.pallas_call(functools.partial(section_kernel, n, videos, parts), out_s...  40.1 us
    unnamed x17, local copies, waits for them, and re-layouts  8.3 us
    slice x2, local copies, waits for them, and re-layouts, section(): return (small[1, 0], dil, head, small[0], inputs)  1.09 us

profile of v1, /device:TPU:0, one launch (start us, length us, event | category | flops | bytes accessed | tf_op | source)
XLA Modules:
  0.0 50.2 jit_solution(7078985118438899232)
XLA Ops:
  0.6 0.0 copy-start
  0.6 1.4 %copy-done = bf16[3,512,512]{2,1,0:T(8,128)(2,1)S(1)} copy-done((bf16[3,512,512]{2,1,0:T(8,128)(2,1)S(1)}, bf16[3,512,512]{2,1,0:T(8,128)(2,1)}, u32[]{:S(2)}) %copy-start) | copy-done | bytes 1572888
  2.0 0.0 copy-start.1
  2.0 0.9 %copy-done.1 = bf16[1,256,512]{2,1,0:T(8,128)(2,1)S(1)} copy-done((bf16[1,256,512]{2,1,0:T(8,128)(2,1)S(1)}, bf16[1,256,512]{2,1,0:T(8,128)(2,1)}, u32[]{:S(2)}) %copy-start.1) | copy-done | bytes 262168
  3.0 0.0 copy-start.2
  3.0 0.9 %copy-done.2 = bf16[512,256]{1,0:T(8,128)(2,1)S(1)} copy-done((bf16[512,256]{1,0:T(8,128)(2,1)S(1)}, bf16[512,256]{1,0:T(8,128)(2,1)}, u32[]{:S(2)}) %copy-start.2) | copy-done | bytes 262168
  3.9 0.0 copy-start.3
  3.9 0.9 %copy-done.3 = bf16[256,256]{1,0:T(8,128)(2,1)S(1)} copy-done((bf16[256,256]{1,0:T(8,128)(2,1)S(1)}, bf16[256,256]{1,0:T(8,128)(2,1)}, u32[]{:S(2)}) %copy-start.3) | copy-done | bytes 131096
  4.8 0.0 copy-start.4
  4.9 0.7 %copy-done.4 = f32[512]{0:T(512)S(1)} copy-done((f32[512]{0:T(512)S(1)}, f32[512]{0:T(512)}, u32[]{:S(2)}) %copy-start.4) | copy-done | bytes 2072
  5.5 0.0 copy-start.5
  5.5 0.7 %copy-done.5 = s32[1,256,2]{1,2,0:T(2,128)S(1)} copy-done((s32[1,256,2]{1,2,0:T(2,128)S(1)}, s32[1,256,2]{1,2,0:T(2,128)}, u32[]{:S(2)}) %copy-start.5) | copy-done | bytes 2072
  6.2 0.0 copy-start.6
  6.2 0.7 %copy-done.6 = s32[4]{0:T(128)S(1)} copy-done((s32[4]{0:T(128)S(1)}, s32[4]{0:T(128)}, u32[]{:S(2)}) %copy-start.6) | copy-done | bytes 40
  6.9 40.1 %shard_map.110 = (f32[3,64,512]{2,1,0:T(8,128)S(1)}, f32[64,256]{1,0:T(8,128)S(1)}, bf16[1,256,512]{2,1,0:T(8,128)(2,1)S(1)}, f32[8,512]{1,0:T(8,128)S(1)}) custom-call(s32[4]{0:T(128)S(1)} %copy-done.6, bf16[1,256,512]{2,1,0:T(8,128)(2,1)S(1)} %copy-done.1, bf16[3,512,512]{2,1,0:T(8,128)(2,1)S(1)} %copy-done, f32[1,512]{1,0:T(1,128)S(1)} %bitcast.6, ...), custom_call_target="tpu_custom_call" | custom-call | tf_op jit(solution)/shard_map/pallas_call | solution.py:477
  47.0 0.6 %slice.7 = f32[1,512]{1,0:T(1,128)} slice(f32[8,512]{1,0:T(8,128)S(1)} %get-tuple-element.9), slice={[0:1], [0:512]} | slice | bytes 4096 | tf_op jit(solution)/shard_map/slice | solution.py:495
  47.6 0.5 %slice.6 = f32[1,1]{1,0:T(1,128)} slice(f32[8,512]{1,0:T(8,128)S(1)} %get-tuple-element.9), slice={[1:2], [0:1]} | slice | bytes 8 | tf_op jit(solution)/shard_map/slice | solution.py:495
  48.1 0.7 %copy.15 = f32[3,64,512]{2,1,0:T(8,128)} copy(f32[3,64,512]{2,1,0:T(8,128)S(1)} %get-tuple-element.19) | data formatting | bytes 786432
  48.8 0.6 %copy.16 = f32[64,256]{1,0:T(8,128)} copy(f32[64,256]{1,0:T(8,128)S(1)} %get-tuple-element.20) | data formatting | bytes 131072
  49.5 0.7 %copy.17 = bf16[1,256,512]{2,1,0:T(8,128)(2,1)} copy(bf16[1,256,512]{2,1,0:T(8,128)(2,1)S(1)} %get-tuple-element.22) | data formatting | bytes 524288
Async XLA Ops:
  0.6 1.4 %copy-start = (bf16[3,512,512]{2,1,0:T(8,128)(2,1)S(1)}, bf16[3,512,512]{2,1,0:T(8,128)(2,1)}, u32[]{:S(2)}) copy-start(bf16[3,512,512]{2,1,0:T(8,128)(2,1)} %weight_ref.1) | copy-start | bytes 4718596
  2.0 0.9 %copy-start.1 = (bf16[1,256,512]{2,1,0:T(8,128)(2,1)S(1)}, bf16[1,256,512]{2,1,0:T(8,128)(2,1)}, u32[]{:S(2)}) copy-start(bf16[1,256,512]{2,1,0:T(8,128)(2,1)} %frames_ref.1) | copy-start | bytes 786436
  3.0 0.9 %copy-start.2 = (bf16[512,256]{1,0:T(8,128)(2,1)S(1)}, bf16[512,256]{1,0:T(8,128)(2,1)}, u32[]{:S(2)}) copy-start(bf16[512,256]{1,0:T(8,128)(2,1)} %head_ref.1) | copy-start | bytes 786436
  3.9 0.9 %copy-start.3 = (bf16[256,256]{1,0:T(8,128)(2,1)S(1)}, bf16[256,256]{1,0:T(8,128)(2,1)}, u32[]{:S(2)}) copy-start(bf16[256,256]{1,0:T(8,128)(2,1)} %narr_ref.1) | copy-start | bytes 393220
  4.8 0.7 %copy-start.4 = (f32[512]{0:T(512)S(1)}, f32[512]{0:T(512)}, u32[]{:S(2)}) copy-start(f32[512]{0:T(512)} %param.9) | copy-start | bytes 6148
  5.5 0.7 %copy-start.5 = (s32[1,256,2]{1,2,0:T(2,128)S(1)}, s32[1,256,2]{1,2,0:T(2,128)}, u32[]{:S(2)}) copy-start(s32[1,256,2]{1,2,0:T(2,128)} %param.13) | copy-start | bytes 6148
  6.2 0.7 %copy-start.6 = (s32[4]{0:T(128)S(1)}, s32[4]{0:T(128)}, u32[]{:S(2)}) copy-start(s32[4]{0:T(128)} %counts_ref.1) | copy-start | bytes 52

commit v2 on v1

--- a/solution.py
+++ b/solution.py
@@ -133,12 +133,24 @@
 
 def section_kernel(
     n, videos, parts,
-    counts_ref, frames_ref, weight_ref, bias_ref, head_ref, narr_ref, spans_ref,
-    dil_ref, head_out_ref, input_ref, small_ref,
+    counts_hbm, frames_hbm, weight_hbm, bias_hbm, head_hbm, narr_hbm, spans_hbm,
+    dil_ref, head_out_ref, input_ref, bias_out_ref, loss_ref,
+    counts_ref, frames_ref, weight_ref, bias_ref, head_ref, narr_ref, spans_ref, load_sem, turned,
     earlier, later, narr_all, spans_all, hidden, out_grad, pre, pre_next, pre_prev,
     small_send, small_recv, edge_send, edge_recv, gather_send, gather_recv,
     small_ssem, small_rsem, *buffers,
 ):
+    loads = [
+        pltpu.make_async_copy(source, target, load_sem.at[k])
+        for k, (source, target) in enumerate(
+            (
+                (frames_hbm, frames_ref), (weight_hbm, weight_ref), (bias_hbm, bias_ref), (spans_hbm, spans_ref),
+                (counts_hbm, counts_ref), (head_hbm, head_ref), (narr_hbm, narr_ref),
+            )
+        )
+    ]
+    for copy in loads:
+        copy.start()
     tm, vid = lax.axis_index("tm"), lax.axis_index("video")
     runs = n // 2
     core, row = lax.rem(vid, 2), lax.div(vid, 2)
@@ -167,16 +179,16 @@
     has_prev, has_next = tm >= SHIFT_N, tm < n - SHIFT_N
     up = {"tm": lax.rem(tm + SHIFT_N, n), "video": vid}
     down = {"tm": lax.rem(tm + n - SHIFT_N, n), "video": vid}
-    frames_up = remote(frames_ref.at[0], earlier, edge_send.at[0], edge_recv.at[0], up)
-    frames_down = remote(frames_ref.at[0], later, edge_send.at[1], edge_recv.at[1], down)
+    frames_up = remote(frames_hbm.at[0], earlier, edge_send.at[0], edge_recv.at[0], up)
+    frames_down = remote(frames_hbm.at[0], later, edge_send.at[1], edge_recv.at[1], down)
     pre_up = remote(pre, pre_prev, edge_send.at[2], edge_recv.at[2], up)
     pre_down = remote(pre, pre_next, edge_send.at[3], edge_recv.at[3], down)
     pl.when(has_next)(frames_up.start)
     pl.when(has_prev)(frames_down.start)
     gathers = []
     for step in range(1, videos):
-        gathers.append(remote(spans_ref, spans_all.at[step - 1], gather_send.at[0, step - 1], gather_recv.at[0, step - 1], at_video(step)))
-        gathers.append(remote(narr_ref, narr_all.at[step - 1], gather_send.at[1, step - 1], gather_recv.at[1, step - 1], at_video(step)))
+        gathers.append(remote(spans_hbm, spans_all.at[step - 1], gather_send.at[0, step - 1], gather_recv.at[0, step - 1], at_video(step)))
+        gathers.append(remote(narr_hbm, narr_all.at[step - 1], gather_send.at[1, step - 1], gather_recv.at[1, step - 1], at_video(step)))
     for copy in gathers:
         copy.start()
 
@@ -191,7 +203,10 @@
     pl.when(jnp.logical_not(has_prev))(no_prev)
     pl.when(jnp.logical_not(has_next))(no_next)
 
+    for copy in loads:
+        copy.wait()
     present = frames_ref[0]
+    turned[...] = present.T
     length = present.shape[0]
     slots_count = narr_ref.shape[0]
     hidden[...] = jnp.dot(present, weight_ref[1], preferred_element_type=F32) + bias_ref[...]
@@ -279,6 +294,8 @@
         for tap, low, high in pieces:
             if tap == 3:
                 values = contracted_rows(layer_out, embed_grad[:, low:high])
+            elif tap == 1:
+                values = jnp.dot(turned[...], pre[:, low:high], preferred_element_type=F32)
             else:
                 values = contracted_rows(taps[tap][...], pre[:, low:high])
             scatter(values, slab, first)
@@ -286,7 +303,7 @@
         first_copies.append(send_first(slab))
 
     bias_local = jnp.sum(pre[...].astype(F32), axis=0, keepdims=True)
-    rows = lax.broadcasted_iota(jnp.int32, small_ref.shape, 0)
+    rows = lax.broadcasted_iota(jnp.int32, small_send.shape[1:], 0)
     small = jnp.where(rows == 0, bias_local, jnp.where(rows == 1, local_loss, 0.0))
     small_copies = []
 
@@ -395,8 +412,8 @@
         for s in range(1, runs):
             term = jnp.where(step == s, small_recv[2 + s], term)
         total_small = term if total_small is None else total_small + term
-    rows = lax.broadcasted_iota(jnp.int32, small_ref.shape, 0)
-    small_ref[...] = jnp.where(rows == 1, total_small / label_total, total_small)
+    bias_out_ref[...] = total_small[0:1]
+    loss_ref[...] = total_small[1:2, 0:1] / label_total
 
     for (pieces, order), slab, copies in zip(parts, slabs, final_copies):
         for step in range(videos):
@@ -427,17 +444,37 @@
             copy.wait_send()
 
 
+def write_kernel(*refs):
+    sems = refs[10]
+    copies = [pltpu.make_async_copy(refs[k], refs[5 + k], sems.at[k]) for k in range(5)]
+    for copy in copies:
+        copy.start()
+    for copy in copies:
+        copy.wait()
+
+
 def section(n, videos, frames, dilated_weight, dilated_bias, head_matrix, narrations, narration_counts, narration_spans):
     length, channels = frames.shape[1:]
     width, slots = head_matrix.shape[1], narrations.shape[0]
     rows, runs = channels // n, n // 2
     band = rows // videos
     half, head_half = channels // 2, width // 2
-    parts = tuple(
-        (tuple((tap, p * half, (p + 1) * half) for tap in range(3)) + ((3, p * head_half, (p + 1) * head_half),), order)
-        for p, order in enumerate(("rows", "sides"))
+    parts = (
+        (((1, 0, channels),), "rows"),
+        (((0, 0, channels),), "sides"),
+        (((2, 0, half), (3, 0, head_half)), "rows"),
+        (((2, half, channels), (3, head_half, width)), "sides"),
     )
     scratch = [
+        pltpu.SMEM((videos,), jnp.int32),
+        pltpu.VMEM((1, length, channels), BF16),
+        pltpu.VMEM((3, channels, channels), BF16),
+        pltpu.VMEM((1, channels), F32),
+        pltpu.VMEM((channels, width), BF16),
+        pltpu.VMEM((slots, width), BF16),
+        pltpu.VMEM((2, slots), jnp.int32),
+        pltpu.SemaphoreType.DMA((7,)),
+        pltpu.VMEM((channels, length), BF16),
         pltpu.VMEM((length, channels), BF16),
         pltpu.VMEM((length, channels), BF16),
         pltpu.VMEM((videos - 1, slots, width), BF16),
@@ -473,26 +510,41 @@
             pltpu.VMEM((band, columns), BF16),
             pltpu.VMEM((videos - 1, band, columns), BF16),
         ]
-    vmem = pl.BlockSpec(memory_space=pltpu.VMEM)
-    dil, head, inputs, small = pl.pallas_call(
+    vmem, hbm = pl.BlockSpec(memory_space=pltpu.VMEM), pl.BlockSpec(memory_space=pltpu.HBM)
+    shapes = (
+        jax.ShapeDtypeStruct((3, rows, channels), F32),
+        jax.ShapeDtypeStruct((rows, width), F32),
+        jax.ShapeDtypeStruct((1, length, channels), BF16),
+        jax.ShapeDtypeStruct((1, channels), F32),
+        jax.ShapeDtypeStruct((1, 1), F32),
+    )
+    results = pl.pallas_call(
         functools.partial(section_kernel, n, videos, parts),
-        out_shape=(
-            jax.ShapeDtypeStruct((3, rows, channels), F32),
-            jax.ShapeDtypeStruct((rows, width), F32),
-            jax.ShapeDtypeStruct((1, length, channels), BF16),
-            jax.ShapeDtypeStruct((8, channels), F32),
-        ),
-        in_specs=[pl.BlockSpec(memory_space=pltpu.SMEM)] + [vmem] * 6,
-        out_specs=(vmem,) * 4,
+        out_shape=shapes,
+        in_specs=[hbm] * 7,
+        out_specs=(vmem,) * 5,
         scratch_shapes=scratch,
         compiler_params=pltpu.CompilerParams(
             collective_id=0, has_side_effects=True, vmem_limit_bytes=48 * 1024 * 1024
         ),
     )(
-        narration_counts, frames, dilated_weight, dilated_bias[None], head_matrix, narrations,
-        narration_spans[0].T,
-    )
-    return small[1, 0], dil, head, small[0], inputs
+        *(
+            pltpu.with_memory_space_constraint(array, pltpu.HBM)
+            for array in (
+                narration_counts, frames, dilated_weight, dilated_bias[None], head_matrix, narrations,
+                narration_spans[0].T,
+            )
+        )
+    )
+    dil, head, inputs, bias, loss = pl.pallas_call(
+        write_kernel,
+        out_shape=shapes,
+        in_specs=[vmem] * 5,
+        out_specs=(hbm,) * 5,
+        scratch_shapes=[pltpu.SemaphoreType.DMA((5,))],
+        compiler_params=pltpu.CompilerParams(vmem_limit_bytes=1024 * 1024),
+    )(*results)
+    return loss[0, 0], dil, head, bias[0], inputs
 
 
 def solution(mesh):

time: 50.4 us -> 39.9 us (0.79)
  local copies, waits for them, and re-layouts: 9.39 us -> 0 us
  Pallas kernels: 40.1 us -> 39.1 us
    unnamed x17 -> x0, local copies, waits for them, and re-layouts: 8.3 us -> none
    pallas_call x1, Pallas kernels: 40.1 us -> 37.6 us  [section(): pl.pallas_call(functools.partial(section_kernel, n, videos, parts), out_s...]
    pallas_call x0 -> x1, Pallas kernels: none -> 1.53 us  [section(): pl.pallas_call(write_kernel, out_shape=shapes, in_specs=[vmem] * 5, out_s...]
    slice x2 -> x0, local copies, waits for them, and re-layouts: 1.09 us -> none  [section(): return (small[1, 0], dil, head, small[0], inputs)]
where the time goes in v2:
time: 39.9 us; the launch traced here: 39.8 us
  Pallas kernels  39.1 us (98%)
  between operations  0.64 us (2%)
    pallas_call x1, Pallas kernels, section(): pl.pallas_call(functools.partial(section_kernel, n, videos, parts), out_s...  37.6 us
    pallas_call x1, Pallas kernels, section(): pl.pallas_call(write_kernel, out_shape=shapes, in_specs=[vmem] * 5, out_s...  1.53 us

profile of v2, /device:TPU:0, one launch (start us, length us, event | category | flops | bytes accessed | tf_op | source)
XLA Modules:
  0.0 39.8 jit_solution(11464504917011683649)
XLA Ops:
  0.6 37.6 %shard_map.110 = (f32[3,64,512]{2,1,0:T(8,128)S(1)}, f32[64,256]{1,0:T(8,128)S(1)}, bf16[1,256,512]{2,1,0:T(8,128)(2,1)S(1)}, f32[1,512]{1,0:T(1,128)S(1)}, f32[1,1]{1,0:T(1,128)}) custom-call(s32[4]{0:T(128)} %counts_hbm.1, bf16[1,256,512]{2,1,0:T(8,128)(2,1)} %frames_hbm.1, bf16[3,512,512]{2,1,0:T(8,128)(2,1)} %weight_hbm.1, f32[1,512]{1,0:T(1,128)} %bitcast.6, ...), custom_call_target="tpu_custom_call" | custom-call | tf_op jit(solution)/shard_map/pallas_call | solution.py:521
  38.3 1.5 %shard_map.111 = (f32[3,64,512]{2,1,0:T(8,128)}, f32[64,256]{1,0:T(8,128)}, bf16[1,256,512]{2,1,0:T(8,128)(2,1)}, f32[1,512]{1,0:T(1,128)}, f32[1,1]{1,0:T(1,128)}) custom-call(f32[3,64,512]{2,1,0:T(8,128)S(1)} %get-tuple-element.15.refs_0_, f32[64,256]{1,0:T(8,128)S(1)} %get-tuple-element.16.refs_1_, bf16[1,256,512]{2,1,0:T(8,128)(2,1)S(1)} %get-tuple-element.17.refs_2_, ...), custom_call_target="tpu_custom_call" | custom-call | tf_op jit(solution)/shard_map/pallas_call | solution.py:539

commit v3 on v2

--- a/solution.py
+++ b/solution.py
@@ -135,7 +135,7 @@
     n, videos, parts,
     counts_hbm, frames_hbm, weight_hbm, bias_hbm, head_hbm, narr_hbm, spans_hbm,
     dil_ref, head_out_ref, input_ref, bias_out_ref, loss_ref,
-    counts_ref, frames_ref, weight_ref, bias_ref, head_ref, narr_ref, spans_ref, load_sem, turned,
+    counts_ref, frames_ref, weight_ref, bias_ref, head_ref, narr_ref, spans_ref, load_sem, turned, layer_out, embed_grad,
     earlier, later, narr_all, spans_all, hidden, out_grad, pre, pre_next, pre_prev,
     small_send, small_recv, edge_send, edge_recv, gather_send, gather_recv,
     small_ssem, small_rsem, *buffers,
@@ -179,12 +179,16 @@
     has_prev, has_next = tm >= SHIFT_N, tm < n - SHIFT_N
     up = {"tm": lax.rem(tm + SHIFT_N, n), "video": vid}
     down = {"tm": lax.rem(tm + n - SHIFT_N, n), "video": vid}
-    frames_up = remote(frames_hbm.at[0], earlier, edge_send.at[0], edge_recv.at[0], up)
-    frames_down = remote(frames_hbm.at[0], later, edge_send.at[1], edge_recv.at[1], down)
-    pre_up = remote(pre, pre_prev, edge_send.at[2], edge_recv.at[2], up)
-    pre_down = remote(pre, pre_next, edge_send.at[3], edge_recv.at[3], down)
-    pl.when(has_next)(frames_up.start)
-    pl.when(has_prev)(frames_down.start)
+    length = frames_hbm.shape[1]
+    half = length // 2
+    blocks = [pl.ds(0, half), pl.ds(half, half)]
+    frames_up = [remote(frames_hbm.at[0, b], earlier.at[b], edge_send.at[k], edge_recv.at[k], up) for k, b in enumerate(blocks)]
+    frames_down = [remote(frames_hbm.at[0, b], later.at[b], edge_send.at[2 + k], edge_recv.at[2 + k], down) for k, b in enumerate(blocks)]
+    pre_up = [remote(pre.at[b], pre_prev.at[b], edge_send.at[4 + k], edge_recv.at[4 + k], up) for k, b in enumerate(blocks)]
+    pre_down = [remote(pre.at[b], pre_next.at[b], edge_send.at[6 + k], edge_recv.at[6 + k], down) for k, b in enumerate(blocks)]
+    for k in range(2):
+        pl.when(has_next)(frames_up[k].start)
+        pl.when(has_prev)(frames_down[k].start)
     gathers = []
     for step in range(1, videos):
         gathers.append(remote(spans_hbm, spans_all.at[step - 1], gather_send.at[0, step - 1], gather_recv.at[0, step - 1], at_video(step)))
@@ -207,65 +211,67 @@
         copy.wait()
     present = frames_ref[0]
     turned[...] = present.T
-    length = present.shape[0]
     slots_count = narr_ref.shape[0]
     hidden[...] = jnp.dot(present, weight_ref[1], preferred_element_type=F32) + bias_ref[...]
     slots = lax.broadcasted_iota(jnp.int32, (1, slots_count), 1)
-    positions = tm * length + lax.broadcasted_iota(jnp.int32, (length, 1), 0)
     starts, ends = spans_ref[0:1, :], spans_ref[1:2, :]
     own_live = slots < counts_ref[vid]
-    member = ((positions >= starts) & (positions < ends) & own_live).astype(F32)
-    labeled = jnp.sum(member, axis=1, keepdims=True)
-
-    def recv_up():
-        frames_up.wait_recv()
-
-    pl.when(has_prev)(recv_up)
-    hidden[...] += jnp.dot(earlier[...], weight_ref[0], preferred_element_type=F32)
-    pl.when(has_next)(frames_down.wait_recv)
-    hidden[...] += jnp.dot(later[...], weight_ref[2], preferred_element_type=F32)
-    layer_out = (present.astype(F32) + jnp.maximum(hidden[...], 0.0)).astype(BF16)
-    embedded = jnp.dot(layer_out, head_ref[...], preferred_element_type=F32).astype(BF16)
-
-    span_sum = jnp.where(own_live, (ends - starts).astype(F32), 0.0)
-    narrs, masked = [], []
-    for step in range(videos):
-        if step:
-            gathers[2 * (step - 1)].wait_recv()
-            gathers[2 * (step - 1) + 1].wait_recv()
-            live = slots < counts_ref[lax.rem(vid + videos - step, videos)]
-            lengths = (spans_all[step - 1, 1:2, :] - spans_all[step - 1, 0:1, :]).astype(F32)
-            span_sum = span_sum + jnp.where(live, lengths, 0.0)
-            table = narr_all[step - 1]
-        else:
-            live, table = own_live, narr_ref[...]
-        narrs.append(table)
-        scores = logit_scale * contracted_columns(embedded, table)
-        if step == 0:
-            own_scores = scores
-        masked.append(jnp.where(live, scores, -jnp.inf))
-    label_total = jnp.sum(span_sum, axis=1, keepdims=True)
-    highest = functools.reduce(jnp.maximum, [jnp.max(m, axis=1, keepdims=True) for m in masked])
-    powers = [jnp.exp(m - highest) for m in masked]
-    total = functools.reduce(jnp.add, [jnp.sum(e, axis=1, keepdims=True) for e in powers])
-    log_total = highest + jnp.log(total)
-    local_loss = jnp.sum(labeled * log_total, axis=0, keepdims=True) - jnp.sum(
-        jnp.sum(member * own_scores, axis=1, keepdims=True), axis=0, keepdims=True
-    )
-    factor = (length * n * videos) / label_total
-    weight = labeled / total
-    embed_sum = None
-    for step in range(videos):
-        probs = powers[step] * weight
-        if step == 0:
-            probs = probs - member
-        term = jnp.dot((probs * factor).astype(BF16), narrs[step], preferred_element_type=F32)
-        embed_sum = term if embed_sum is None else embed_sum + term
-    embed_grad = (logit_scale * embed_sum).astype(BF16)
-    out_grad[...] = contracted_columns(embed_grad, head_ref[...]).astype(BF16)
-    pre[...] = jnp.where(hidden[...] > 0.0, out_grad[...].astype(F32), 0.0).astype(BF16)
-    pl.when(has_next)(pre_up.start)
-    pl.when(has_prev)(pre_down.start)
+    lives = [own_live] + [slots < counts_ref[lax.rem(vid + videos - step, videos)] for step in range(1, videos)]
+    local_loss = None
+    for k, block in enumerate(blocks):
+        positions = tm * length + k * half + lax.broadcasted_iota(jnp.int32, (half, 1), 0)
+        member = ((positions >= starts) & (positions < ends) & own_live).astype(F32)
+        labeled = jnp.sum(member, axis=1, keepdims=True)
+        pl.when(has_prev)(frames_up[k].wait_recv)
+        pl.when(has_next)(frames_down[k].wait_recv)
+        state = (
+            hidden[block]
+            + jnp.dot(earlier[block], weight_ref[0], preferred_element_type=F32)
+            + jnp.dot(later[block], weight_ref[2], preferred_element_type=F32)
+        )
+        layer = (frames_ref[0, block].astype(F32) + jnp.maximum(state, 0.0)).astype(BF16)
+        layer_out[block] = layer
+        embedded = jnp.dot(layer, head_ref[...], preferred_element_type=F32).astype(BF16)
+        if k == 0:
+            span_sum = jnp.where(own_live, (ends - starts).astype(F32), 0.0)
+            for step in range(1, videos):
+                gathers[2 * (step - 1)].wait_recv()
+                gathers[2 * (step - 1) + 1].wait_recv()
+                lengths = (spans_all[step - 1, 1:2, :] - spans_all[step - 1, 0:1, :]).astype(F32)
+                span_sum = span_sum + jnp.where(lives[step], lengths, 0.0)
+            label_total = jnp.sum(span_sum, axis=1, keepdims=True)
+            factor = (length * n * videos) / label_total
+        masked = []
+        for step in range(videos):
+            table = narr_all[step - 1] if step else narr_ref[...]
+            scores = logit_scale * contracted_columns(embedded, table)
+            if step == 0:
+                own_scores = scores
+            masked.append(jnp.where(lives[step], scores, -jnp.inf))
+        highest = functools.reduce(jnp.maximum, [jnp.max(m, axis=1, keepdims=True) for m in masked])
+        powers = [jnp.exp(m - highest) for m in masked]
+        total = functools.reduce(jnp.add, [jnp.sum(e, axis=1, keepdims=True) for e in powers])
+        log_total = highest + jnp.log(total)
+        part_loss = jnp.sum(labeled * log_total, axis=0, keepdims=True) - jnp.sum(
+            jnp.sum(member * own_scores, axis=1, keepdims=True), axis=0, keepdims=True
+        )
+        local_loss = part_loss if local_loss is None else local_loss + part_loss
+        share = labeled / total
+        embed_sum = None
+        for step in range(videos):
+            probs = powers[step] * share
+            if step == 0:
+                probs = probs - member
+            table = narr_all[step - 1] if step else narr_ref[...]
+            term = jnp.dot((probs * factor).astype(BF16), table, preferred_element_type=F32)
+            embed_sum = term if embed_sum is None else embed_sum + term
+        embed = (logit_scale * embed_sum).astype(BF16)
+        embed_grad[block] = embed
+        gradient = contracted_columns(embed, head_ref[...]).astype(BF16)
+        out_grad[block] = gradient
+        pre[block] = jnp.where(state > 0.0, gradient.astype(F32), 0.0).astype(BF16)
+        pl.when(has_next)(pre_up[k].start)
+        pl.when(has_prev)(pre_down[k].start)
 
     taps = (earlier, frames_ref.at[0], later)
     slabs = [buffers[13 * p:13 * (p + 1)] for p in range(len(parts))]
@@ -293,7 +299,7 @@
         first = 0
         for tap, low, high in pieces:
             if tap == 3:
-                values = contracted_rows(layer_out, embed_grad[:, low:high])
+                values = contracted_rows(layer_out[...], embed_grad[:, low:high])
             elif tap == 1:
                 values = jnp.dot(turned[...], pre[:, low:high], preferred_element_type=F32)
             else:
@@ -340,9 +346,11 @@
     small_now = small_start(1, [across_row])
 
     grad = out_grad[...].astype(F32) + contracted_columns(pre[...], weight_ref[1])
-    pl.when(has_prev)(pre_up.wait_recv)
+    for copy in pre_up:
+        pl.when(has_prev)(copy.wait_recv)
     grad = grad + contracted_columns(pre_prev[...], weight_ref[2])
-    pl.when(has_next)(pre_down.wait_recv)
+    for copy in pre_down:
+        pl.when(has_next)(copy.wait_recv)
     grad = grad + contracted_columns(pre_next[...], weight_ref[0])
     input_ref[0] = grad.astype(BF16)
 
@@ -433,10 +441,10 @@
                     dil_ref[tap, at, low:high] = piece
                 first += high - low
 
-    pl.when(has_next)(frames_up.wait_send)
-    pl.when(has_prev)(frames_down.wait_send)
-    pl.when(has_next)(pre_up.wait_send)
-    pl.when(has_prev)(pre_down.wait_send)
+    for copy in frames_up + pre_up:
+        pl.when(has_next)(copy.wait_send)
+    for copy in frames_down + pre_down:
+        pl.when(has_prev)(copy.wait_send)
     for copy in gathers + first_copies + small_copies + second_copies + third_copies:
         copy.wait_send()
     for started in run_copies + final_copies:
@@ -476,6 +484,8 @@
         pltpu.SemaphoreType.DMA((7,)),
         pltpu.VMEM((channels, length), BF16),
         pltpu.VMEM((length, channels), BF16),
+        pltpu.VMEM((length, width), BF16),
+        pltpu.VMEM((length, channels), BF16),
         pltpu.VMEM((length, channels), BF16),
         pltpu.VMEM((videos - 1, slots, width), BF16),
         pltpu.VMEM((videos - 1, 2, slots), jnp.int32),
@@ -486,8 +496,8 @@
         pltpu.VMEM((length, channels), BF16),
         pltpu.VMEM((4, 8, channels), F32),
         pltpu.VMEM((2 + runs, 8, channels), F32),
-        pltpu.SemaphoreType.DMA((4,)),
-        pltpu.SemaphoreType.DMA((4,)),
+        pltpu.SemaphoreType.DMA((8,)),
+        pltpu.SemaphoreType.DMA((8,)),
         pltpu.SemaphoreType.DMA((2, videos - 1)),
         pltpu.SemaphoreType.DMA((2, videos - 1)),
         pltpu.SemaphoreType.DMA((2 + runs,)),

time: 39.9 us -> 39.2 us (0.982)
  Pallas kernels: 39.1 us -> 38.4 us
    pallas_call x1, Pallas kernels: 37.6 us -> 36.9 us  [section(): pl.pallas_call(functools.partial(section_kernel, n, videos, parts), out_s...]
where the time goes in v3:
time: 39.2 us; the launch traced here: 39 us
  Pallas kernels  38.4 us (98%)
  between operations  0.64 us (2%)
    pallas_call x1, Pallas kernels, section(): pl.pallas_call(functools.partial(section_kernel, n, videos, parts), out_s...  36.9 us
    pallas_call x1, Pallas kernels, section(): pl.pallas_call(write_kernel, out_shape=shapes, in_specs=[vmem] * 5, out_s...  1.53 us

profile of v3, /device:TPU:0, one launch (start us, length us, event | category | flops | bytes accessed | tf_op | source)
XLA Modules:
  0.0 39.0 jit_solution(1010099554608859896)
XLA Ops:
  0.6 36.9 %shard_map.110 = (f32[3,64,512]{2,1,0:T(8,128)S(1)}, f32[64,256]{1,0:T(8,128)S(1)}, bf16[1,256,512]{2,1,0:T(8,128)(2,1)S(1)}, f32[1,512]{1,0:T(1,128)S(1)}, f32[1,1]{1,0:T(1,128)}) custom-call(s32[4]{0:T(128)} %counts_hbm.1, bf16[1,256,512]{2,1,0:T(8,128)(2,1)} %frames_hbm.1, bf16[3,512,512]{2,1,0:T(8,128)(2,1)} %weight_hbm.1, f32[1,512]{1,0:T(1,128)} %bitcast.6, ...), custom_call_target="tpu_custom_call" | custom-call | tf_op jit(solution)/shard_map/pallas_call | solution.py:531
  37.5 1.5 %shard_map.111 = (f32[3,64,512]{2,1,0:T(8,128)}, f32[64,256]{1,0:T(8,128)}, bf16[1,256,512]{2,1,0:T(8,128)(2,1)}, f32[1,512]{1,0:T(1,128)}, f32[1,1]{1,0:T(1,128)}) custom-call(f32[3,64,512]{2,1,0:T(8,128)S(1)} %get-tuple-element.15.refs_0_, f32[64,256]{1,0:T(8,128)S(1)} %get-tuple-element.16.refs_1_, bf16[1,256,512]{2,1,0:T(8,128)(2,1)S(1)} %get-tuple-element.17.refs_2_, ...), custom_call_target="tpu_custom_call" | custom-call | tf_op jit(solution)/shard_map/pallas_call | solution.py:549
